TPU v7x, 32 devices: a whole 2x2x4 slice. The times are simulated.
32 devices in a mesh: pole: 4 (over y, x), row: 8 (over z, core).
Axes of the slice: x: 2, y: 2, z: 4, core: 2. Of those that a mesh axis runs over, the one named last changes fastest.
Arguments:
- basis: bfloat16 [32768, 128], P('row'), may hold values from -24 to 24
- inverses: bfloat16 [4, 64, 512, 512], P('pole', 'row'), may hold values from -1.5 to 1.5
- lower: bfloat16 [64, 512, 512], P('row'), may hold values from -0.03955078 to 0.03955078
- upper: bfloat16 [64, 512, 512], P('row'), may hold values from -0.03955078 to 0.03955078
- pole_weights: float32 [4], P('pole'), may hold values from 0.5 to 1.5
Outputs:
- new_basis: float32 [32768, 128], P(('row', 'pole'))
All inputs are finite; a program needn't handle non-finite values.
Results may differ from a plain program's by a relative error of at most 0.003.
Values may be sent and summed in bfloat16 or wider, within the bound.
A program may use at most 64 MiB of HBM per device.

v0:
```python
import jax
import jax.numpy as jnp
from jax import lax
from jax.sharding import PartitionSpec as P

SWEEPS = 4


def padded_2(value, sides, width):
    for axis, dim in sides:
        peers, length = (lax.axis_size(axis), value.shape[dim])
        up = [(i, (i + 1) % peers) for i in range(peers - 1)]
        down = [(j, i) for i, j in up]
        last = lax.slice_in_dim(value, length - width, length, axis=dim)
        initial = lax.slice_in_dim(value, 0, width, axis=dim)
        before = lax.ppermute(last, axis, up)
        after = lax.ppermute(initial, axis, down)
        value = jnp.concatenate([before, value, after], axis=dim)
    return value


def shards(basis, inverses, lower, upper, pole_weights):
    rows, width = basis.shape
    count = inverses.shape[1]
    size = inverses.shape[-1]
    inverse = inverses[0]
    blocks = basis.reshape(count, size, width)
    state = jnp.einsum("bij,bjk->bik", inverse, blocks, preferred_element_type=jnp.float32).astype(
        jnp.bfloat16
    )
    for sweep in range(SWEEPS):
        padded = padded_2(state.reshape(rows, width), (("row", 0),), size)
        padded = padded.reshape(count + 2, size, width)
        rhs = blocks.astype(jnp.float32)
        rhs = rhs + jnp.einsum(
            "bij,bjk->bik", lower, padded[:-2], preferred_element_type=jnp.float32
        )
        rhs = rhs + jnp.einsum(
            "bij,bjk->bik", upper, padded[2:], preferred_element_type=jnp.float32
        )
        state = jnp.einsum(
            "bij,bjk->bik", inverse, rhs.astype(jnp.bfloat16), preferred_element_type=jnp.float32
        ).astype(jnp.bfloat16)
    weighted = pole_weights[0] * state.reshape(rows, width).astype(jnp.float32)
    total_rows = rows * lax.axis_size("row")
    filtered = lax.psum(weighted, "pole")
    share = rows // lax.axis_size("pole")
    mine = lax.dynamic_slice_in_dim(filtered, lax.axis_index("pole") * share, share, 0)
    partial_gram = jnp.dot(filtered.T, filtered, precision=lax.Precision.HIGHEST)
    gram = lax.psum(partial_gram, "row")
    gram = gram / total_rows
    factor = jnp.linalg.cholesky(gram)
    solved = jax.scipy.linalg.solve_triangular(factor, mine.T, lower=True)
    return solved.T


def solution(mesh):
    return jax.shard_map(
        shards,
        mesh=mesh,
        in_specs=(
            P("row", None),
            P("pole", "row", None, None),
            P("row", None, None),
            P("row", None, None),
            P("pole"),
        ),
        out_specs=P(("row", "pole"), None),
        check_vma=False,
    )
```

profile of v0, /device:TPU:0, one launch (start us, length us, event | category | flops | bytes accessed | tf_op | source)
XLA Modules:
  0.0 268.5 jit_solution(1977090597358284194)
XLA Ops:
  6.5 3.8 %fusion.18 = bf16[8,512,128]{2,1,0:T(8,128)(2,1)S(1)} fusion(bf16[8,512,128]{2,1,0:T(8,128)(2,1)} %bitcast.142, bf16[1,8,512,512]{3,2,1,0:T(8,128)(2,1)} %param.6), kind=kOutput, calls=%fused_computation.23 | convolution fusion | flops 537395200 | bytes 6291456 | tf_op jit(solution)/shard_map/bij,bjk->bik/dot_general | solution.py:28
  10.4 2.4 collective-permute-start
  14.7 3.7 %collective-permute-done.1 = bf16[512,128]{1,0:T(8,128)(2,1)} collective-permute-done((bf16[512,128]{1,0:T(8,128)(2,1)S(1)}, bf16[512,128]{1,0:T(8,128)(2,1)}, u32[]{:S(2)}, u32[]{:S(2)}) %collective-permute-start.1) | collective-permute-done | bytes 131104 | tf_op jit(solution)/shard_map/ppermute | solution.py:17
  18.4 2.0 pad_maximum_fusion.6
  20.4 3.7 %fusion.50 = f32[8,128,512]{2,1,0:T(8,128)S(1)} fusion(bf16[8,512,128]{2,1,0:T(8,128)(2,1)S(1)} %bitcast.131, bf16[8,512,512]{2,1,0:T(8,128)(2,1)} %param.7), kind=kOutput, calls=%fused_computation.60 | convolution fusion | flops 536870912 | bytes 7340032 | tf_op jit(solution)/shard_map/bij,bjk->bik/dot_general | solution.py:35
  24.1 7.6 %fusion.41 = bf16[8,512,128]{1,2,0:T(8,128)(2,1)} fusion(bf16[1,8,512,512]{3,2,1,0:T(8,128)(2,1)} %param.6, bf16[8,512,128]{1,2,0:T(8,128)(2,1)S(1)} %copy.15, f32[8,128,512]{2,1,0:T(8,128)S(1)} %fusion.50, bf16[8,512,128]{2,1,0:T(8,128)(2,1)} %bitcast.138, bf16[8,512,512]{2,1,0:T(8,128)(2,1)} %param.8), kind=kOutput, calls=%fused_computation.30 | convolution fusion | flops 1076363264 | bytes 13631488 | tf_op jit(solution)/shard_map/bij,bjk->bik/dot_general | solution.py:41
  32.7 5.4 %collective-permute-start.2 = (bf16[512,128]{0,1:T(8,128)(2,1)S(1)}, bf16[512,128]{0,1:T(8,128)(2,1)S(1)}, u32[]{:S(2)}, u32[]{:S(2)}) collective-permute-start(bf16[512,128]{0,1:T(8,128)(2,1)S(1)} %get-tuple-element.16), channel_id=1, source_target_pairs={{0,1},{1,2},{2,3},{3,4},{4,5},{5,6},{6,7},{8,9},{9,10},{10,11},{11... | collective-permute-start | bytes 393224 | tf_op jit(solution)/shard_map/ppermute | solution.py:16
  39.4 1.6 copy.16
  42.6 3.7 %fusion.51 = f32[8,128,512]{2,1,0:T(8,128)S(1)} fusion(bf16[8,512,128]{2,1,0:T(8,128)(2,1)S(1)} %bitcast.132, bf16[8,512,512]{2,1,0:T(8,128)(2,1)} %param.7), kind=kOutput, calls=%fused_computation.61 | convolution fusion | flops 536870912 | bytes 7340032 | tf_op jit(solution)/shard_map/bij,bjk->bik/dot_general | solution.py:35
  46.3 7.6 %fusion.38 = bf16[8,512,128]{1,2,0:T(8,128)(2,1)} fusion(bf16[1,8,512,512]{3,2,1,0:T(8,128)(2,1)} %param.6, bf16[8,512,128]{1,2,0:T(8,128)(2,1)S(1)} %copy.15, f32[8,128,512]{2,1,0:T(8,128)S(1)} %fusion.51, bf16[8,512,128]{2,1,0:T(8,128)(2,1)} %bitcast.139, bf16[8,512,512]{2,1,0:T(8,128)(2,1)} %param.8), kind=kOutput, calls=%fused_computation.29 | convolution fusion | flops 1076363264 | bytes 13631488 | tf_op jit(solution)/shard_map/bij,bjk->bik/dot_general | solution.py:41
  55.0 5.0 %collective-permute-start.4 = (bf16[512,128]{0,1:T(8,128)(2,1)S(1)}, bf16[512,128]{0,1:T(8,128)(2,1)S(1)}, u32[]{:S(2)}, u32[]{:S(2)}) collective-permute-start(bf16[512,128]{0,1:T(8,128)(2,1)S(1)} %get-tuple-element.12), channel_id=1, source_target_pairs={{0,1},{1,2},{2,3},{3,4},{4,5},{5,6},{6,7},{8,9},{9,10},{10,11},{11... | collective-permute-start | bytes 393224 | tf_op jit(solution)/shard_map/ppermute | solution.py:16
  61.2 1.6 copy.19
  64.4 3.7 %fusion.52 = f32[8,128,512]{2,1,0:T(8,128)S(1)} fusion(bf16[8,512,128]{2,1,0:T(8,128)(2,1)S(1)} %bitcast.133, bf16[8,512,512]{2,1,0:T(8,128)(2,1)} %param.7), kind=kOutput, calls=%fused_computation.62 | convolution fusion | flops 536870912 | bytes 7340032 | tf_op jit(solution)/shard_map/bij,bjk->bik/dot_general | solution.py:35
  68.1 7.6 %fusion.35 = bf16[8,512,128]{1,2,0:T(8,128)(2,1)} fusion(bf16[1,8,512,512]{3,2,1,0:T(8,128)(2,1)} %param.6, bf16[8,512,128]{1,2,0:T(8,128)(2,1)S(1)} %copy.15, f32[8,128,512]{2,1,0:T(8,128)S(1)} %fusion.52, bf16[8,512,128]{2,1,0:T(8,128)(2,1)} %bitcast.140, bf16[8,512,512]{2,1,0:T(8,128)(2,1)} %param.8), kind=kOutput, calls=%fused_computation.28 | convolution fusion | flops 1076363264 | bytes 13631488 | tf_op jit(solution)/shard_map/bij,bjk->bik/dot_general | solution.py:41
  76.7 5.0 %collective-permute-start.6 = (bf16[512,128]{0,1:T(8,128)(2,1)S(1)}, bf16[512,128]{0,1:T(8,128)(2,1)S(1)}, u32[]{:S(2)}, u32[]{:S(2)}) collective-permute-start(bf16[512,128]{0,1:T(8,128)(2,1)S(1)} %get-tuple-element.8), channel_id=1, source_target_pairs={{0,1},{1,2},{2,3},{3,4},{4,5},{5,6},{6,7},{8,9},{9,10},{10,11},{11... | collective-permute-start | bytes 393224 | tf_op jit(solution)/shard_map/ppermute | solution.py:16
  86.9 3.7 %fusion.53 = f32[8,128,512]{2,1,0:T(8,128)S(1)} fusion(bf16[8,512,128]{2,1,0:T(8,128)(2,1)S(1)} %bitcast.134, bf16[8,512,512]{2,1,0:T(8,128)(2,1)} %param.7), kind=kOutput, calls=%fused_computation.63 | convolution fusion | flops 536870912 | bytes 7340032 | tf_op jit(solution)/shard_map/bij,bjk->bik/dot_general | solution.py:35
  90.6 8.0 %multiply_bitcast_fusion = f32[8,512,128]{1,2,0:T(8,128)} fusion(bf16[1,8,512,512]{3,2,1,0:T(8,128)(2,1)} %param.6, bf16[8,512,128]{1,2,0:T(8,128)(2,1)S(1)} %copy.15, f32[8,128,512]{2,1,0:T(8,128)S(1)} %fusion.53, bf16[8,512,128]{2,1,0:T(8,128)(2,1)} %bitcast.130, bf16[8,512,512]{2,1,0:T(8,128)(2,1)} %param.8, f32[]{:T(128)} %bitcast.128), kind=kOutput, calls=%fused_computation.22 | convolution fusion | flops 1077411840 | bytes 14680068 | tf_op jit(solution)/shard_map/bij,bjk->bik/dot_general | solution.py:41
  98.5 2.9 %copy.25 = f32[8,512,128]{2,1,0:T(8,128)} copy(f32[8,512,128]{1,2,0:T(8,128)} %multiply_bitcast_fusion) | data formatting | bytes 4194304 | tf_op jit(solution)/shard_map/mul | solution.py:44
  101.5 71.8 %all-reduce.3.cloned.1.call-done = f32[4096,128]{1,0:T(8,128)} async-done(((f32[4096,128]{1,0:T(8,128)}), f32[4096,128]{1,0:T(8,128)}) %all-reduce.3.cloned.1.call-update) | async-done | bytes 2097168 | tf_op jit(solution)/shard_map/psum | solution.py:46
  173.4 6.3 %fusion.54 = f32[128,128]{0,1:T(8,128)} fusion(f32[4096,128]{1,0:T(8,128)} %all-reduce.3.cloned.1.call-done), kind=kOutput, calls=%fused_computation.64 | convolution fusion | flops 805306368 | bytes 2162688 | tf_op jit(solution)/shard_map/dot_general | solution.py:49
  179.7 54.8 %all-reduce.5.cloned.1.call-done = f32[128,128]{0,1:T(8,128)} async-done(((f32[128,128]{0,1:T(8,128)}), f32[128,128]{0,1:T(8,128)}) %all-reduce.5.cloned.1.call-update) | async-done | bytes 65552 | tf_op jit(solution)/shard_map/psum | solution.py:50
  236.3 11.7 %cholesky.16 = f32[128,128]{1,0:T(8,128)S(1)} custom-call(f32[128,128]{1,0:T(8,128)S(1)} %fusion.48), custom_call_target="Cholesky" | custom-call | tf_op jit(solution)/shard_map/jit(cholesky)/cholesky | solution.py:52
  249.4 9.8 %custom-call.7 = f32[1,128,128]{1,2,0:T(8,128)S(1)} custom-call(f32[1,128,128]{2,1,0:T(8,128)S(1)} %fusion.46), custom_call_target="InvertDiagBlocksLowerTriangular" | custom-call | tf_op jit(solution)/shard_map/jit(_solve_triangular)/triangular_solve | solution.py:53
  259.2 2.4 fusion.44
  (38 shorter events, 18.1 us)
Async XLA Ops:
  6.5 166.8 %all-reduce.3.cloned.1.call-start = ((), (), s32[]{:S(2)}) async-start(), calls=%async_computation | async-start | bytes 4194304 | tf_op jit(solution)/shard_map/psum | solution.py:46
  6.5 7.6 %copy-start = (bf16[4096,128]{1,0:T(8,128)(2,1)S(1)}, bf16[4096,128]{1,0:T(8,128)(2,1)}, u32[]{:S(2)}) copy-start(bf16[4096,128]{1,0:T(8,128)(2,1)} %param.5) | copy-start | bytes 3145732
  10.4 4.3 %collective-permute-start = (bf16[512,128]{1,0:T(8,128)(2,1)S(1)}, bf16[512,128]{1,0:T(8,128)(2,1)S(1)}, u32[]{:S(2)}, u32[]{:S(2)}) collective-permute-start(bf16[512,128]{1,0:T(8,128)(2,1)S(1)} %get-tuple-element.20), channel_id=1, source_target_pairs={{0,1},{1,2},{2,3},{3,4},{4,5},{5,6},{6,7},{8,9},{9,10},{10,11},{11... | collective-permute-start | bytes 393224 | tf_op jit(solution)/shard_map/ppermute | solution.py:16
  12.8 5.5 %collective-permute-start.1 = (bf16[512,128]{1,0:T(8,128)(2,1)S(1)}, bf16[512,128]{1,0:T(8,128)(2,1)}, u32[]{:S(2)}, u32[]{:S(2)}) collective-permute-start(bf16[512,128]{1,0:T(8,128)(2,1)S(1)} %get-tuple-element.19), channel_id=1, source_target_pairs={{1,0},{2,1},{3,2},{4,3},{5,4},{6,5},{7,6},{9,8},{10,9},{11,10},{12... | collective-permute-start | bytes 393224 | tf_op jit(solution)/shard_map/ppermute | solution.py:17
  32.7 8.4 %collective-permute-start.2 = (bf16[512,128]{0,1:T(8,128)(2,1)S(1)}, bf16[512,128]{0,1:T(8,128)(2,1)S(1)}, u32[]{:S(2)}, u32[]{:S(2)}) collective-permute-start(bf16[512,128]{0,1:T(8,128)(2,1)S(1)} %get-tuple-element.16), channel_id=1, source_target_pairs={{0,1},{1,2},{2,3},{3,4},{4,5},{5,6},{6,7},{8,9},{9,10},{10,11},{11... | collective-permute-start | bytes 393224 | tf_op jit(solution)/shard_map/ppermute | solution.py:16
  38.1 3.2 %collective-permute-start.3 = (bf16[512,128]{0,1:T(8,128)(2,1)S(1)}, bf16[512,128]{0,1:T(8,128)(2,1)S(1)}, u32[]{:S(2)}, u32[]{:S(2)}) collective-permute-start(bf16[512,128]{0,1:T(8,128)(2,1)S(1)} %get-tuple-element.15), channel_id=1, source_target_pairs={{1,0},{2,1},{3,2},{4,3},{5,4},{6,5},{7,6},{9,8},{10,9},{11,10},{12... | collective-permute-start | bytes 393224 | tf_op jit(solution)/shard_map/ppermute | solution.py:17
  55.0 7.9 %collective-permute-start.4 = (bf16[512,128]{0,1:T(8,128)(2,1)S(1)}, bf16[512,128]{0,1:T(8,128)(2,1)S(1)}, u32[]{:S(2)}, u32[]{:S(2)}) collective-permute-start(bf16[512,128]{0,1:T(8,128)(2,1)S(1)} %get-tuple-element.12), channel_id=1, source_target_pairs={{0,1},{1,2},{2,3},{3,4},{4,5},{5,6},{6,7},{8,9},{9,10},{10,11},{11... | collective-permute-start | bytes 393224 | tf_op jit(solution)/shard_map/ppermute | solution.py:16
  59.9 3.2 %collective-permute-start.5 = (bf16[512,128]{0,1:T(8,128)(2,1)S(1)}, bf16[512,128]{0,1:T(8,128)(2,1)S(1)}, u32[]{:S(2)}, u32[]{:S(2)}) collective-permute-start(bf16[512,128]{0,1:T(8,128)(2,1)S(1)} %get-tuple-element.11), channel_id=1, source_target_pairs={{1,0},{2,1},{3,2},{4,3},{5,4},{6,5},{7,6},{9,8},{10,9},{11,10},{12... | collective-permute-start | bytes 393224 | tf_op jit(solution)/shard_map/ppermute | solution.py:17
  76.7 8.7 %collective-permute-start.6 = (bf16[512,128]{0,1:T(8,128)(2,1)S(1)}, bf16[512,128]{0,1:T(8,128)(2,1)S(1)}, u32[]{:S(2)}, u32[]{:S(2)}) collective-permute-start(bf16[512,128]{0,1:T(8,128)(2,1)S(1)} %get-tuple-element.8), channel_id=1, source_target_pairs={{0,1},{1,2},{2,3},{3,4},{4,5},{5,6},{6,7},{8,9},{9,10},{10,11},{11... | collective-permute-start | bytes 393224 | tf_op jit(solution)/shard_map/ppermute | solution.py:16
  81.7 3.9 %collective-permute-start.7 = (bf16[512,128]{0,1:T(8,128)(2,1)S(1)}, bf16[512,128]{0,1:T(8,128)(2,1)S(1)}, u32[]{:S(2)}, u32[]{:S(2)}) collective-permute-start(bf16[512,128]{0,1:T(8,128)(2,1)S(1)} %get-tuple-element.7), channel_id=1, source_target_pairs={{1,0},{2,1},{3,2},{4,3},{5,4},{6,5},{7,6},{9,8},{10,9},{11,10},{12... | collective-permute-start | bytes 393224 | tf_op jit(solution)/shard_map/ppermute | solution.py:17
  101.5 133.1 %all-reduce.5.cloned.1.call-start = ((), (), s32[]{:S(2)}) async-start(), calls=%async_computation.1 | async-start | bytes 131072 | tf_op jit(solution)/shard_map/psum | solution.py:50
Sparse Core Ops, SparseCore 0:
  101.6 71.7 all-reduce.2
  179.8 54.6 all-reduce.4
where the time goes:
time: 269 us; the launch traced here: 268 us
  waiting for transfers between devices  131 us (49%)
  matrix products  58.2 us (22%)
  other arithmetic  29.9 us (11%)
  starting transfers between devices  23.2 us (9%)
  between operations  14.3 us (5%)
  local copies, waits for them, and re-layouts  12.1 us (4%)
    psum x1, waiting for transfers between devices, shards(): filtered = lax.psum(weighted, 'pole')  71.8 us
    psum x1, waiting for transfers between devices, shards(): gram = lax.psum(partial_gram, 'row')  54.8 us
    dot_general x4, matrix products, shards(): jnp.einsum('bij,bjk->bik', inverse, rhs.astype(jnp.bfloat16), preferred_e...  30.9 us
    ppermute x4, starting transfers between devices, padded_2(): before = lax.ppermute(last, axis, up)  17.8 us
    dot_general x4, matrix products, shards(): jnp.einsum('bij,bjk->bik', lower, padded[:-2], preferred_element_type=jnp...  14.8 us
    another operation x3, other arithmetic, shards(): factor = jnp.linalg.cholesky(gram)  12.4 us
    another operation x2, other arithmetic, shards(): solved = jax.scipy.linalg.solve_triangular(factor, mine.T, lower=True)  10.5 us
    dot_general x1, matrix products, shards(): jnp.dot(filtered.T, filtered, precision=lax.Precision.HIGHEST)  6.31 us
  transfers between devices with their start and end apart: 10, of which 5 were waited for; matrix products, arithmetic and copies ran while one was open for 2% of the time, Pallas kernels for 0%

commit v1 on v0

v1 whole, which is shorter than its diff:
```python
import functools

import jax
import jax.numpy as jnp
from jax import lax
from jax.experimental import pallas as pl
from jax.experimental.pallas import tpu as pltpu
from jax.sharding import PartitionSpec as P

SWEEPS = 4
MESH = pl.DeviceIdType.MESH
F32 = jnp.float32
BF16 = jnp.bfloat16
HIGHEST = lax.Precision.HIGHEST


def dot(a, b):
    return jnp.dot(a, b, preferred_element_type=F32)


def sweep_kernel(
    poles,
    rings,
    weight_ref,
    basis_hbm,
    inverse_hbm,
    lower_hbm,
    upper_hbm,
    mine_ref,
    gram_ref,
    basis,
    inverse,
    lower,
    upper,
    states,
    weights,
    got,
    partial,
    shares,
    piece,
    pieces,
    whole,
    load_sem,
    halo_send,
    halo_recv,
    weight_send,
    weight_recv,
    final_send,
    final_recv,
    share_send,
    share_recv,
    piece_send,
    piece_recv,
    whole_send,
    whole_recv,
):
    pole, row = lax.axis_index("pole"), lax.axis_index("row")
    count, size, width = basis.shape
    owned = count // poles
    pairs = count // 2
    has_left, has_right = row > 0, row < rings - 1

    def load(kind, b):
        source = (basis_hbm, inverse_hbm, lower_hbm, upper_hbm)[kind]
        target = (basis, inverse, lower, upper)[kind]
        return pltpu.make_async_copy(source.at[b], target.at[b], load_sem.at[kind, b])

    def send(src, dst, send_sem, recv_sem, **where):
        return pltpu.make_async_remote_copy(
            src_ref=src,
            dst_ref=dst,
            send_sem=send_sem,
            recv_sem=recv_sem,
            device_id=where,
            device_id_type=MESH,
        )

    for i in range(count):
        b = (i - 1) % count
        load(0, b).start()
        load(1, b).start()
    for i in range(count):
        b = (i + 1) % count
        load(2, b).start()
        load(3, b).start()

    weights[pole] = jnp.full(weights.shape[1:], weight_ref[0], F32)
    zero = jnp.zeros((size, width), BF16)

    @pl.when(jnp.logical_not(has_left))
    def _():
        for k in range(SWEEPS):
            states[k, 0] = zero

    @pl.when(jnp.logical_not(has_right))
    def _():
        for k in range(SWEEPS):
            states[k, count + 1] = zero

    barrier = pltpu.get_barrier_semaphore()
    for d in range(1, poles):
        pl.semaphore_signal(barrier, inc=1, device_id={"pole": lax.rem(pole + d, poles)}, device_id_type=MESH)
    for d in range(1, rings):
        pl.semaphore_signal(barrier, inc=1, device_id={"row": lax.rem(row + d, rings)}, device_id_type=MESH)

    def to_left(k):
        return send(
            states.at[k, 1], states.at[k, count + 1], halo_send.at[k, 0], halo_recv.at[k, 0], row=row - 1
        )

    def to_right(k):
        return send(states.at[k, count], states.at[k, 0], halo_send.at[k, 1], halo_recv.at[k, 1], row=row + 1)

    def send_halos(k):
        @pl.when(has_left)
        def _():
            to_left(k).start()

        @pl.when(has_right)
        def _():
            to_right(k).start()

    def first(i, carry):
        blocks = [lax.rem(2 * i + count - 1, count), lax.rem(2 * i, count)]
        for b in blocks:
            load(0, b).wait()
            load(1, b).wait()
        for b in blocks:
            states[0, b + 1] = dot(inverse[b], basis[b]).astype(BF16)

        @pl.when(i == 0)
        def _():
            pl.semaphore_wait(barrier, poles + rings - 2)
            send_halos(0)

        return carry

    lax.fori_loop(0, pairs, first, 0)

    for d in range(1, poles):
        send(
            weights.at[pole],
            weights.at[pole],
            weight_send.at[d],
            weight_recv.at[pole],
            pole=lax.rem(pole + d, poles),
        ).start()

    def final(b):
        return send(
            states.at[SWEEPS, b + 1],
            got.at[pole, lax.rem(b, owned)],
            final_send.at[b],
            final_recv.at[pole, lax.rem(b, owned)],
            pole=b // owned,
        )

    def sweep(t, carry):
        k = t // pairs + 1
        i = lax.rem(t, pairs)
        blocks = [lax.rem(2 * i + 1, count), lax.rem(2 * i + 2, count)]

        @pl.when(k == 1)
        def _():
            for b in blocks:
                load(2, b).wait()
                load(3, b).wait()

        @pl.when(jnp.logical_and(i == pairs - 1, has_left))
        def _():
            to_right(k - 1).wait_recv()

        @pl.when(jnp.logical_and(i == pairs - 1, has_right))
        def _():
            to_left(k - 1).wait_recv()

        for b in blocks:
            rhs = basis[b].astype(F32) + dot(lower[b], states[k - 1, b])
            rhs = rhs + dot(upper[b], states[k - 1, b + 2])
            states[k, b + 1] = dot(inverse[b], rhs.astype(BF16)).astype(BF16)

        @pl.when(jnp.logical_and(i == pairs - 1, k < SWEEPS))
        def _():
            send_halos(k)

        for b in blocks:

            @pl.when(jnp.logical_and(k == SWEEPS, b // owned != pole))
            def _():
                final(b).start()

        return carry

    lax.fori_loop(0, SWEEPS * pairs, sweep, 0)

    def weighted(p, block):
        return block.astype(F32) * weights[p, 0:1, :]

    others = [lax.rem(pole + d, poles) for d in range(1, poles)]
    for p in others:
        send(
            weights.at[p], weights.at[p], weight_send.at[0], weight_recv.at[p], pole=p
        ).wait_recv()
    total = jnp.zeros((width, width), F32)
    for j in range(owned):
        block = weighted(pole, states[SWEEPS, pole * owned + j + 1])
        for p in others:
            send(
                got.at[p, j], got.at[p, j], final_send.at[0], final_recv.at[p, j], pole=p
            ).wait_recv()
            block = block + weighted(p, got[p, j])
        mine_ref[j * size : (j + 1) * size, :] = block
        total = total + lax.dot_general(
            block, block, (((0,), (0,)), ((), ())), precision=HIGHEST, preferred_element_type=F32
        )

    lines = width // poles
    for q in range(poles):
        partial[q] = total[q * lines : (q + 1) * lines, :]

    def share_to(d):
        q = lax.rem(pole + d, poles)
        return send(partial.at[q], shares.at[pole], share_send.at[d], share_recv.at[pole], pole=q)

    for d in range(1, poles):
        share_to(d).start()
    part = partial[pole]
    for p in others:
        send(shares.at[p], shares.at[p], share_send.at[0], share_recv.at[p], pole=p).wait_recv()
        part = part + shares[p]
    piece[...] = part

    def piece_to(d):
        q = lax.rem(row + d, rings)
        return send(piece, pieces.at[row], piece_send.at[d], piece_recv.at[row], row=q)

    for d in range(1, rings):
        piece_to(d).start()
    for d in range(1, rings):
        p = lax.rem(row + d, rings)
        send(pieces.at[p], pieces.at[p], piece_send.at[0], piece_recv.at[p], row=p).wait_recv()
        part = part + pieces[p]
    whole[pole] = part

    def whole_to(d):
        q = lax.rem(pole + d, poles)
        return send(whole.at[pole], whole.at[pole], whole_send.at[d], whole_recv.at[pole], pole=q)

    for d in range(1, poles):
        whole_to(d).start()
    for p in others:
        send(whole.at[p], whole.at[p], whole_send.at[0], whole_recv.at[p], pole=p).wait_recv()
    scale = 1.0 / (count * size * rings)
    for q in range(poles):
        gram_ref[q * lines : (q + 1) * lines, :] = whole[q] * scale

    for k in range(SWEEPS):

        @pl.when(has_left)
        def _():
            to_left(k).wait_send()

        @pl.when(has_right)
        def _():
            to_right(k).wait_send()

    for b in range(count):

        @pl.when(b // owned != pole)
        def _():
            final(b).wait_send()

    for d in range(1, poles):
        send(
            weights.at[pole], weights.at[pole], weight_send.at[d], weight_recv.at[pole], pole=lax.rem(pole + d, poles)
        ).wait_send()
        share_to(d).wait_send()
        whole_to(d).wait_send()
    for d in range(1, rings):
        piece_to(d).wait_send()


def sweeps_and_gram(basis, inverse, lower, upper, pole_weights):
    poles, rings = lax.axis_size("pole"), lax.axis_size("row")
    count, size, width = basis.shape
    owned = count // poles
    lines = width // poles
    dma = pltpu.SemaphoreType.DMA
    anywhere = pl.BlockSpec(memory_space=pl.ANY)
    return pl.pallas_call(
        functools.partial(sweep_kernel, poles, rings),
        out_shape=(
            jax.ShapeDtypeStruct((owned * size, width), F32),
            jax.ShapeDtypeStruct((width, width), F32),
        ),
        in_specs=[pl.BlockSpec(memory_space=pltpu.SMEM)] + [anywhere] * 4,
        out_specs=(pl.BlockSpec(memory_space=pltpu.VMEM),) * 2,
        scratch_shapes=[
            pltpu.VMEM((count, size, width), BF16),
            pltpu.VMEM((count, size, size), BF16),
            pltpu.VMEM((count, size, size), BF16),
            pltpu.VMEM((count, size, size), BF16),
            pltpu.VMEM((SWEEPS + 1, count + 2, size, width), BF16),
            pltpu.VMEM((poles, 8, width), F32),
            pltpu.VMEM((poles, owned, size, width), BF16),
            pltpu.VMEM((poles, lines, width), F32),
            pltpu.VMEM((poles, lines, width), F32),
            pltpu.VMEM((lines, width), F32),
            pltpu.VMEM((rings, lines, width), F32),
            pltpu.VMEM((poles, lines, width), F32),
            dma((4, count)),
            dma((SWEEPS, 2)),
            dma((SWEEPS, 2)),
            dma((poles,)),
            dma((poles,)),
            dma((count,)),
            dma((poles, owned)),
            dma((poles,)),
            dma((poles,)),
            dma((rings,)),
            dma((rings,)),
            dma((poles,)),
            dma((poles,)),
        ],
        compiler_params=pltpu.CompilerParams(collective_id=0, has_side_effects=True),
        name="sweeps",
    )(pole_weights, basis, inverse, lower, upper)


def shards(basis, inverses, lower, upper, pole_weights):
    rows, width = basis.shape
    count, size = inverses.shape[1], inverses.shape[-1]
    mine, gram = sweeps_and_gram(
        basis.reshape(count, size, width), inverses[0], lower, upper, pole_weights
    )
    factor = jnp.linalg.cholesky(gram)
    solved = jax.scipy.linalg.solve_triangular(factor, mine.T, lower=True)
    return solved.T


def solution(mesh):
    return jax.shard_map(
        shards,
        mesh=mesh,
        in_specs=(
            P("row", None),
            P("pole", "row", None, None),
            P("row", None, None),
            P("row", None, None),
            P("pole"),
        ),
        out_specs=P(("row", "pole"), None),
        check_vma=False,
    )
```

time: 269 us -> 90.7 us (0.34)
  waiting for transfers between devices: 131 us -> 0 us
  Pallas kernels: 0 us -> 62.7 us
  matrix products: 58.2 us -> 2.4 us
  starting transfers between devices: 23.2 us -> 0 us
  between operations: 14.3 us -> 0.69 us
  local copies, waits for them, and re-layouts: 12.1 us -> 0.93 us
  other arithmetic: 29.9 us -> 23.7 us
    psum x2 -> x0, waiting for transfers between devices: 127 us -> none  [the longest x1 71.8 us: shards(): filtered = lax.psum(weighted, 'pole')]
    pallas_call x0 -> x1, Pallas kernels: none -> 62.7 us  [sweeps_and_gram(): pl.pallas_call(functools.partial(sweep_kernel, poles, rings), out_shape=(...]
    dot_general x10 -> x0, matrix products: 55.8 us -> none  [the longest x4 30.9 us: shards(): jnp.einsum('bij,bjk->bik', inverse, rhs.astype(jnp.bfloat16), preferred_e...]
    ppermute x8 -> x0, starting transfers between devices: 23.1 us -> none  [the longest x4 17.8 us: padded_2(): before = lax.ppermute(last, axis, up)]
    concatenate x4 -> x0, other arithmetic: 5.36 us -> none  [padded_2(): value = jnp.concatenate([before, value, after], axis=dim)]
    convert_element_type x3 -> x0, local copies, waits for them, and re-layouts: 4.85 us -> none  [shards(): state = jnp.einsum('bij,bjk->bik', inverse, rhs.astype(jnp.bfloat16), pre...]
    ppermute x8 -> x0, waiting for transfers between devices: 4.07 us -> none  [the longest x4 4.06 us: padded_2(): after = lax.ppermute(initial, axis, down)]
    slice x4 -> x0, local copies, waits for them, and re-layouts: 2.97 us -> none  [padded_2(): initial = lax.slice_in_dim(value, 0, width, axis=dim)]
  transfers between devices with their start and end apart: 10 -> 0, of which waited for: 5 -> 0; matrix products, arithmetic and copies ran while one was open for 2% -> 0% of each run, Pallas kernels for 0% -> 0%
where the time goes in v1:
time: 90.7 us; the launch traced here: 90.4 us
  Pallas kernels  62.7 us (69%)
  other arithmetic  23.7 us (26%)
  matrix products  2.4 us (3%)
  local copies, waits for them, and re-layouts  0.93 us (1%)
    pallas_call x1, Pallas kernels, sweeps_and_gram(): pl.pallas_call(functools.partial(sweep_kernel, poles, rings), out_shape=(...  62.7 us
    another operation x3, other arithmetic, shards(): factor = jnp.linalg.cholesky(gram)  12.4 us
    another operation x2, other arithmetic, shards(): solved = jax.scipy.linalg.solve_triangular(factor, mine.T, lower=True)  10.5 us
    another operation x1, matrix products, shards(): solved = jax.scipy.linalg.solve_triangular(factor, mine.T, lower=True)  2.4 us

profile of v1, /device:TPU:0, one launch (start us, length us, event | category | flops | bytes accessed | tf_op | source)
XLA Modules:
  0.0 90.4 jit_solution(6013619810335207867)
XLA Ops:
  0.7 62.7 %sweeps.1 = (f32[1024,128]{1,0:T(8,128)}, f32[128,128]{1,0:T(8,128)}) custom-call(f32[1]{0:T(128)S(6)} %copy.7.weight_ref, bf16[8,512,128]{2,1,0:T(8,128)(2,1)} %bitcast.13, bf16[8,512,512]{2,1,0:T(8,128)(2,1)} %bitcast.12, bf16[8,512,512]{2,1,0:T(8,128)(2,1)} %lower_hbm.1, bf16[8,512,512]{2,1,0:T(8,128)(2,1)} %upper_hbm.1), custom_call_target="tpu_custom_call" | custom-call | tf_op jit(solution)/shard_map/sweeps/pallas_call | solution.py:290
  63.4 0.9 %copy.6 = f32[128,128]{0,1:T(8,128)S(1)} copy(f32[128,128]{1,0:T(8,128)} %get-tuple-element.8) | data formatting | bytes 131072 | tf_op jit(solution)/shard_map/sweeps/pallas_call | solution.py:290
  64.3 0.9 fusion.3
  65.2 11.7 %cholesky.16 = f32[128,128]{1,0:T(8,128)S(1)} custom-call(f32[128,128]{1,0:T(8,128)S(1)} %fusion.3), custom_call_target="Cholesky" | custom-call | tf_op jit(solution)/shard_map/jit(cholesky)/cholesky | solution.py:336
  76.9 0.6 compare_reduce_fusion
  77.6 0.7 fusion
  78.2 9.8 %custom-call.7 = f32[1,128,128]{1,2,0:T(8,128)S(1)} custom-call(f32[1,128,128]{2,1,0:T(8,128)S(1)} %fusion), custom_call_target="InvertDiagBlocksLowerTriangular" | custom-call | tf_op jit(solution)/shard_map/jit(_solve_triangular)/triangular_solve | solution.py:337
  88.0 2.4 %fusion.1 = f32[1024,128]{1,0:T(8,128)} fusion(f32[1024,128]{1,0:T(8,128)} %get-tuple-element.7, f32[1,128,128]{1,2,0:T(8,128)S(1)} %custom-call.7), kind=kOutput, calls=%fused_computation.2 | convolution fusion | flops 201326592 | bytes 1114112 | tf_op jit(solution)/shard_map/jit(_solve_triangular)/triangular_solve | solution.py:337
  (1 shorter events, 0.0 us)

commit v2 on v1

--- a/solution.py
+++ b/solution.py
@@ -327,15 +327,70 @@
     )(pole_weights, basis, inverse, lower, upper)
 
 
+def inverse_factor(gram):
+    n = gram.shape[0]
+    lane = lax.broadcasted_iota(jnp.int32, (8, n), 1)
+    sub = lax.broadcasted_iota(jnp.int32, (8, n), 0)
+    lane1 = lane[0:1]
+    rows = [gram[g:g+8] for g in range(0, n, 8)]
+    for g in range(n // 8):
+        base = 8 * g
+        t = rows[g]
+        cols = [jnp.broadcast_to(t[:, base+k:base+k+1], (8, n)) for k in range(8)]
+        ratios, tops = {}, []
+        for k in range(8):
+            inv = 1.0 / cols[k][k:k+1]
+            top = jnp.where(lane1 == base + k, inv, t[k:k+1] * inv)
+            below = jnp.where(sub > k, cols[k], 0.0)
+            t = jnp.where((lane == base + k) & (sub > k), 0.0, t) - below * top
+            for l in range(k+1, 8):
+                ratios[k, l] = cols[l][k:k+1] * inv
+                cols[l] = cols[l] - below * ratios[k, l]
+            tops.append(jnp.where((lane1 > base + k) & (lane1 < base + 8), 0.0, top))
+        rows[g] = t
+        inside = (lane >= base) & (lane < base + 8)
+        for h in range(g+1, n // 8):
+            t = rows[h]
+            c = [jnp.broadcast_to(t[:, base+k:base+k+1], (8, n)) for k in range(8)]
+            t = jnp.where(inside, 0.0, t)
+            for k in range(8):
+                t = t - c[k] * tops[k]
+                for l in range(k+1, 8):
+                    c[l] = c[l] - c[k] * ratios[k, l]
+            rows[h] = t
+    out = []
+    for g, t in enumerate(rows):
+        row = sub + 8 * g
+        root = lax.rsqrt(jnp.sum(jnp.where(lane == row, t, 0.0), axis=1, keepdims=True))
+        out.append(jnp.where(lane < row, t, jnp.where(lane == row, 1.0, 0.0)) * root)
+    return jnp.concatenate(out, axis=0)
+
+
+def solve_kernel(mine_ref, gram_ref, out_ref):
+    inverse = inverse_factor(gram_ref[...])
+    out_ref[...] = lax.dot_general(
+        mine_ref[...], inverse, (((1,), (1,)), ((), ())), precision=HIGHEST, preferred_element_type=F32
+    )
+
+
+def orthonormalize(mine, gram):
+    vmem = pl.BlockSpec(memory_space=pltpu.VMEM)
+    return pl.pallas_call(
+        solve_kernel,
+        out_shape=jax.ShapeDtypeStruct(mine.shape, F32),
+        in_specs=[vmem] * 2,
+        out_specs=vmem,
+        name="orthonormalize",
+    )(mine, gram)
+
+
 def shards(basis, inverses, lower, upper, pole_weights):
     rows, width = basis.shape
     count, size = inverses.shape[1], inverses.shape[-1]
     mine, gram = sweeps_and_gram(
         basis.reshape(count, size, width), inverses[0], lower, upper, pole_weights
     )
-    factor = jnp.linalg.cholesky(gram)
-    solved = jax.scipy.linalg.solve_triangular(factor, mine.T, lower=True)
-    return solved.T
+    return orthonormalize(mine, gram)
 
 
 def solution(mesh):

time: 90.7 us -> 69.2 us (0.76)
  other arithmetic: 23.7 us -> 0 us
  Pallas kernels: 62.7 us -> 68.3 us
  matrix products: 2.4 us -> 0 us
  local copies, waits for them, and re-layouts: 0.93 us -> 0 us
    another operation x5 -> x0, other arithmetic: 22.9 us -> none  [the longest x3 12.4 us: shards(): factor = jnp.linalg.cholesky(gram)]
    pallas_call x0 -> x1, Pallas kernels: none -> 5.62 us  [orthonormalize(): pl.pallas_call(solve_kernel, out_shape=jax.ShapeDtypeStruct(mine.shape, F...]
    another operation x1 -> x0, matrix products: 2.4 us -> none  [shards(): solved = jax.scipy.linalg.solve_triangular(factor, mine.T, lower=True)]
    pallas_call x1 -> x0, local copies, waits for them, and re-layouts: 0.93 us -> none  [sweeps_and_gram(): pl.pallas_call(functools.partial(sweep_kernel, poles, rings), out_shape=(...]
where the time goes in v2:
time: 69.2 us; the launch traced here: 69 us
  Pallas kernels  68.3 us (99%)
    pallas_call x1, Pallas kernels, sweeps_and_gram(): pl.pallas_call(functools.partial(sweep_kernel, poles, rings), out_shape=(...  62.7 us
    pallas_call x1, Pallas kernels, orthonormalize(): pl.pallas_call(solve_kernel, out_shape=jax.ShapeDtypeStruct(mine.shape, F...  5.62 us

profile of v2, /device:TPU:0, one launch (start us, length us, event | category | flops | bytes accessed | tf_op | source)
XLA Modules:
  0.0 69.0 jit_solution(9789012445428618704)
XLA Ops:
  0.7 62.7 %sweeps.1 = (f32[1024,128]{1,0:T(8,128)}, f32[128,128]{1,0:T(8,128)}) custom-call(f32[1]{0:T(128)S(6)} %copy.6.weight_ref, bf16[8,512,128]{2,1,0:T(8,128)(2,1)} %bitcast.3, bf16[8,512,512]{2,1,0:T(8,128)(2,1)} %bitcast.2, bf16[8,512,512]{2,1,0:T(8,128)(2,1)} %lower_hbm.1, bf16[8,512,512]{2,1,0:T(8,128)(2,1)} %upper_hbm.1), custom_call_target="tpu_custom_call" | custom-call | tf_op jit(solution)/shard_map/sweeps/pallas_call | solution.py:290
  63.4 5.6 %orthonormalize.1 = f32[1024,128]{1,0:T(8,128)} custom-call(f32[1024,128]{1,0:T(8,128)} %get-tuple-element.7.mine_ref, f32[128,128]{1,0:T(8,128)} %get-tuple-element.8.gram_ref), custom_call_target="tpu_custom_call" | custom-call | tf_op jit(solution)/shard_map/orthonormalize/pallas_call | solution.py:378

commit v3 on v2

--- a/solution.py
+++ b/solution.py
@@ -57,7 +57,6 @@
     pole, row = lax.axis_index("pole"), lax.axis_index("row")
     count, size, width = basis.shape
     owned = count // poles
-    pairs = count // 2
     has_left, has_right = row > 0, row < rings - 1
 
     def load(kind, b):
@@ -120,22 +119,18 @@
         def _():
             to_right(k).start()
 
-    def first(i, carry):
-        blocks = [lax.rem(2 * i + count - 1, count), lax.rem(2 * i, count)]
+    edge = sorted({0, count - 1})
+    inner = list(range(1, count - 1))
+    for blocks in [edge] + [inner[j : j + 3] for j in range(0, len(inner), 3)]:
         for b in blocks:
             load(0, b).wait()
             load(1, b).wait()
-        for b in blocks:
-            states[0, b + 1] = dot(inverse[b], basis[b]).astype(BF16)
-
-        @pl.when(i == 0)
-        def _():
+        starts = [dot(inverse[b], basis[b]).astype(BF16) for b in blocks]
+        for b, start in zip(blocks, starts):
+            states[0, b + 1] = start
+        if blocks is edge:
             pl.semaphore_wait(barrier, poles + rings - 2)
             send_halos(0)
-
-        return carry
-
-    lax.fori_loop(0, pairs, first, 0)
 
     for d in range(1, poles):
         send(
@@ -149,49 +144,73 @@
     def final(b):
         return send(
             states.at[SWEEPS, b + 1],
-            got.at[pole, lax.rem(b, owned)],
+            got.at[pole, b % owned],
             final_send.at[b],
-            final_recv.at[pole, lax.rem(b, owned)],
+            final_recv.at[pole, b % owned],
             pole=b // owned,
         )
 
-    def sweep(t, carry):
-        k = t // pairs + 1
-        i = lax.rem(t, pairs)
-        blocks = [lax.rem(2 * i + 1, count), lax.rem(2 * i + 2, count)]
-
-        @pl.when(k == 1)
-        def _():
-            for b in blocks:
-                load(2, b).wait()
-                load(3, b).wait()
-
-        @pl.when(jnp.logical_and(i == pairs - 1, has_left))
-        def _():
-            to_right(k - 1).wait_recv()
-
-        @pl.when(jnp.logical_and(i == pairs - 1, has_right))
-        def _():
-            to_left(k - 1).wait_recv()
-
+    def below(k, b):
+        return dot(lower[b], states[k - 1, b])
+
+    def above(k, b):
+        return dot(upper[b], states[k - 1, b + 2])
+
+    def send_finals(blocks):
         for b in blocks:
-            rhs = basis[b].astype(F32) + dot(lower[b], states[k - 1, b])
-            rhs = rhs + dot(upper[b], states[k - 1, b + 2])
-            states[k, b + 1] = dot(inverse[b], rhs.astype(BF16)).astype(BF16)
-
-        @pl.when(jnp.logical_and(i == pairs - 1, k < SWEEPS))
-        def _():
-            send_halos(k)
-
-        for b in blocks:
-
-            @pl.when(jnp.logical_and(k == SWEEPS, b // owned != pole))
+
+            @pl.when(b // owned != pole)
             def _():
                 final(b).start()
 
+    def sweep(k, groups, loading=False, last=False):
+        for blocks in groups:
+            if loading:
+                for b in blocks:
+                    load(2, b).wait()
+                    load(3, b).wait()
+            sides = [(basis[b].astype(F32) + below(k, b) + above(k, b)).astype(BF16) for b in blocks]
+            if blocks is groups[-1]:
+                if loading:
+                    for b in edge:
+                        load(2, b).wait()
+                        load(3, b).wait()
+                head = basis[0].astype(F32) + above(k, 0)
+                tail = basis[count - 1].astype(F32) + below(k, count - 1)
+            fresh = [dot(inverse[b], side).astype(BF16) for b, side in zip(blocks, sides)]
+            for b, value in zip(blocks, fresh):
+                states[k, b + 1] = value
+            if last:
+                send_finals(blocks)
+
+        @pl.when(has_left)
+        def _():
+            to_right(k - 1).wait_recv()
+
+        @pl.when(has_right)
+        def _():
+            to_left(k - 1).wait_recv()
+
+        head = (head + below(k, 0)).astype(BF16)
+        tail = (tail + above(k, count - 1)).astype(BF16)
+        head = dot(inverse[0], head).astype(BF16)
+        tail = dot(inverse[count - 1], tail).astype(BF16)
+        states[k, 1] = head
+        states[k, count] = tail
+        if last:
+            send_finals(edge)
+        else:
+            send_halos(k)
+
+    halves = [inner[: len(inner) // 2], inner[len(inner) // 2 :]]
+    sweep(1, halves, loading=True)
+
+    def middle(k, carry):
+        sweep(k, [inner])
         return carry
 
-    lax.fori_loop(0, SWEEPS * pairs, sweep, 0)
+    lax.fori_loop(2, SWEEPS, middle, 0)
+    sweep(SWEEPS, halves, last=True)
 
     def weighted(p, block):
         return block.astype(F32) * weights[p, 0:1, :]

time: 69.2 us -> 55.2 us (0.80)
  Pallas kernels: 68.3 us -> 54.4 us
    pallas_call x1, Pallas kernels: 62.7 us -> 48.8 us  [sweeps_and_gram(): pl.pallas_call(functools.partial(sweep_kernel, poles, rings), out_shape=(...]
where the time goes in v3:
time: 55.2 us; the launch traced here: 55 us
  Pallas kernels  54.4 us (99%)
  between operations  0.66 us (1%)
    pallas_call x1, Pallas kernels, sweeps_and_gram(): pl.pallas_call(functools.partial(sweep_kernel, poles, rings), out_shape=(...  48.8 us
    pallas_call x1, Pallas kernels, orthonormalize(): pl.pallas_call(solve_kernel, out_shape=jax.ShapeDtypeStruct(mine.shape, F...  5.62 us

profile of v3, /device:TPU:0, one launch (start us, length us, event | category | flops | bytes accessed | tf_op | source)
XLA Modules:
  0.0 55.0 jit_solution(13866512552728044859)
XLA Ops:
  0.7 48.8 %sweeps.1 = (f32[1024,128]{1,0:T(8,128)}, f32[128,128]{1,0:T(8,128)}) custom-call(f32[1]{0:T(128)S(6)} %copy.6.weight_ref, bf16[8,512,128]{2,1,0:T(8,128)(2,1)} %bitcast.3, bf16[8,512,512]{2,1,0:T(8,128)(2,1)} %bitcast.2, bf16[8,512,512]{2,1,0:T(8,128)(2,1)} %lower_hbm.1, bf16[8,512,512]{2,1,0:T(8,128)(2,1)} %upper_hbm.1), custom_call_target="tpu_custom_call" | custom-call | tf_op jit(solution)/shard_map/sweeps/pallas_call | solution.py:309
  49.4 5.6 %orthonormalize.1 = f32[1024,128]{1,0:T(8,128)} custom-call(f32[1024,128]{1,0:T(8,128)} %get-tuple-element.7.mine_ref, f32[128,128]{1,0:T(8,128)} %get-tuple-element.8.gram_ref), custom_call_target="tpu_custom_call" | custom-call | tf_op jit(solution)/shard_map/orthonormalize/pallas_call | solution.py:397

commit v4 on v3

--- a/solution.py
+++ b/solution.py
@@ -163,7 +163,7 @@
             def _():
                 final(b).start()
 
-    def sweep(k, groups, loading=False, last=False):
+    def sweep(k, groups, loading=False, last=False, between=None):
         for blocks in groups:
             if loading:
                 for b in blocks:
@@ -182,6 +182,8 @@
                 states[k, b + 1] = value
             if last:
                 send_finals(blocks)
+        if between is not None:
+            between()
 
         @pl.when(has_left)
         def _():
@@ -209,8 +211,20 @@
         sweep(k, [inner])
         return carry
 
-    lax.fori_loop(2, SWEEPS, middle, 0)
-    sweep(SWEEPS, halves, last=True)
+    lax.fori_loop(2, SWEEPS - 1, middle, 0)
+
+    def ends(blocks):
+        sides = [(basis[b].astype(F32) + below(SWEEPS, b) + above(SWEEPS, b)).astype(BF16) for b in blocks]
+        fresh = [dot(inverse[b], side).astype(BF16) for b, side in zip(blocks, sides)]
+        for b, value in zip(blocks, fresh):
+            states[SWEEPS, b + 1] = value
+        send_finals(blocks)
+
+    core = inner[2:-2]
+    sweep(SWEEPS - 1, [inner], between=lambda: ends(core))
+    rest = [b for b in inner if b not in core]
+    outer = [b for b in rest if b in (inner[0], inner[-1])]
+    sweep(SWEEPS, [outer, [b for b in rest if b not in outer]], last=True)
 
     def weighted(p, block):
         return block.astype(F32) * weights[p, 0:1, :]

time: 55.2 us -> 54.1 us (0.980)
  Pallas kernels: 54.4 us -> 53.3 us
    pallas_call x1, Pallas kernels: 48.8 us -> 47.6 us  [sweeps_and_gram(): pl.pallas_call(functools.partial(sweep_kernel, poles, rings), out_shape=(...]
where the time goes in v4:
time: 54.1 us; the launch traced here: 53.9 us
  Pallas kernels  53.3 us (99%)
  between operations  0.66 us (1%)
    pallas_call x1, Pallas kernels, sweeps_and_gram(): pl.pallas_call(functools.partial(sweep_kernel, poles, rings), out_shape=(...  47.6 us
    pallas_call x1, Pallas kernels, orthonormalize(): pl.pallas_call(solve_kernel, out_shape=jax.ShapeDtypeStruct(mine.shape, F...  5.62 us

profile of v4, /device:TPU:0, one launch (start us, length us, event | category | flops | bytes accessed | tf_op | source)
XLA Modules:
  0.0 53.9 jit_solution(17283952571919971643)
XLA Ops:
  0.7 47.6 %sweeps.1 = (f32[1024,128]{1,0:T(8,128)}, f32[128,128]{1,0:T(8,128)}) custom-call(f32[1]{0:T(128)S(6)} %copy.6.weight_ref, bf16[8,512,128]{2,1,0:T(8,128)(2,1)} %bitcast.3, bf16[8,512,512]{2,1,0:T(8,128)(2,1)} %bitcast.2, bf16[8,512,512]{2,1,0:T(8,128)(2,1)} %lower_hbm.1, bf16[8,512,512]{2,1,0:T(8,128)(2,1)} %upper_hbm.1), custom_call_target="tpu_custom_call" | custom-call | tf_op jit(solution)/shard_map/sweeps/pallas_call | solution.py:323
  48.3 5.6 %orthonormalize.1 = f32[1024,128]{1,0:T(8,128)} custom-call(f32[1024,128]{1,0:T(8,128)} %get-tuple-element.7.mine_ref, f32[128,128]{1,0:T(8,128)} %get-tuple-element.8.gram_ref), custom_call_target="tpu_custom_call" | custom-call | tf_op jit(solution)/shard_map/orthonormalize/pallas_call | solution.py:411
